TPU v7x, 256 devices: a whole 4x4x8 slice. The times are simulated.
256 devices in a mesh: dp: 8 (over z), row: 8 (over y_hi, x), col: 4 (over y_lo, core).
Axes of the slice: x: 4, y: 4 (y_hi: 2, y_lo: 2; y = y_hi * 2 + y_lo), z: 8, core: 2. Of those that a mesh axis runs over, the one named last changes fastest.
Arguments:
- inputs: bfloat16 [8, 192, 64, 512], P('dp', None, 'row', 'col'), may hold values from -16 to 16
- norm_gain: float32 [192], replicated, may hold values from 0.25 to 1.75
- w_expand: bfloat16 [192, 768], replicated, may hold values from -0.4375 to 0.4375
- kernel: float32 [768, 9], replicated, may hold values from -2 to 2
- w_squeeze: float32 [768, 48], replicated, may hold values from -1.5 to 1.5
- w_excite: float32 [48, 768], replicated, may hold values from -6 to 6
- w_project: bfloat16 [768, 192], replicated, may hold values from -0.21875 to 0.21875
- cotangent: bfloat16 [8, 192, 64, 512], P('dp', None, 'row', 'col'), may hold values from -16 to 16
Outputs:
- output: bfloat16 [8, 192, 64, 512], P('dp', None, 'row', 'col')
- grad_inputs: bfloat16 [8, 192, 64, 512], P('dp', None, 'row', 'col')
- grad_gain: float32 [192], replicated
- grad_w_expand: float32 [192, 768], replicated
- grad_kernel: float32 [768, 9], replicated
- grad_w_squeeze: float32 [768, 48], replicated
- grad_w_excite: float32 [48, 768], replicated
- grad_w_project: float32 [768, 192], replicated
All inputs are finite; a program needn't handle non-finite values.
Results may differ from a plain program's by a relative error of at most 0.0019.
Values may be sent and summed in bfloat16 or wider, within the bound.
No kernel may reach another device: no remote copies, remote signals or barrier semaphores. Data moves between devices by JAX's collectives and lax.ppermute only.
A program may use at most 64 MiB of HBM per device.

v0:
```python
import jax
import jax.numpy as jnp
from jax import lax
from jax.sharding import PartitionSpec as P

EPS = 1e-06
HIGH = lax.Precision.HIGHEST


def with_halo(shard, sides, width):
    for axis, dim in sides:
        count, length = (lax.axis_size(axis), shard.shape[dim])
        up = [(i, (i + 1) % count) for i in range(count - 1)]
        down = [(j, i) for i, j in up]
        last = lax.slice_in_dim(shard, length - width, length, axis=dim)
        leading = lax.slice_in_dim(shard, 0, width, axis=dim)
        before = lax.ppermute(last, axis, up)
        after = lax.ppermute(leading, axis, down)
        shard = jnp.concatenate([before, shard, after], axis=dim)
    return shard


def silu_slope(value):
    sig = jax.nn.sigmoid(value)
    return sig * (1.0 + value * (1.0 - sig))


def normalize(inputs, norm_gain):
    widened = inputs.astype(jnp.float32)
    inverse = lax.rsqrt(jnp.mean(widened * widened, axis=1, keepdims=True) + EPS)
    normed = widened * inverse
    scaled = (normed * norm_gain[None, :, None, None]).astype(jnp.bfloat16)
    return (normed, inverse, scaled)


def expand(scaled, w_expand):
    return jnp.einsum("bchw,ce->behw", scaled, w_expand, preferred_element_type=jnp.float32)


def depthwise(hidden_pad, kernel, out_rows, out_cols):
    total = jnp.zeros((hidden_pad.shape[0], hidden_pad.shape[1], out_rows, out_cols), jnp.float32)
    for tap in range(9):
        drow, dcol = (tap // 3, tap % 3)
        total = (
            total
            + kernel[:, tap][None, :, None, None]
            * hidden_pad[:, :, drow : drow + out_rows, dcol : dcol + out_cols]
        )
    return total


def local(inputs, norm_gain, w_expand, kernel, w_squeeze, w_excite, w_project, cotangent):
    batch, chans, rows, cols = inputs.shape
    pixels = rows * cols * lax.axis_size("row") * lax.axis_size("col")
    normed, inverse, scaled = normalize(inputs, norm_gain)
    pre = expand(scaled, w_expand)
    hidden = jax.nn.silu(pre).astype(jnp.bfloat16)
    hidden_pad = with_halo(hidden, (("row", 2), ("col", 3)), 1)
    conv = depthwise(hidden_pad, kernel, rows, cols)
    act = jax.nn.silu(conv)
    pooled = lax.psum(jnp.sum(act, axis=(2, 3)), ("row", "col")) / pixels
    squeeze_pre = jnp.dot(pooled, w_squeeze, precision=HIGH)
    squeezed = jax.nn.silu(squeeze_pre)
    excite_pre = jnp.dot(squeezed, w_excite, precision=HIGH)
    excite = jax.nn.sigmoid(excite_pre)
    gated = (act * excite[:, :, None, None]).astype(jnp.bfloat16)
    proj = jnp.einsum("behw,ec->bchw", gated, w_project, preferred_element_type=jnp.float32)
    output = (inputs.astype(jnp.float32) + proj).astype(jnp.bfloat16)
    grad_gated = jnp.einsum(
        "bchw,ec->behw", cotangent, w_project, preferred_element_type=jnp.float32
    )
    grad_project = jnp.einsum("behw,bchw->ec", gated, cotangent, preferred_element_type=jnp.float32)
    grad_excite = lax.psum(jnp.sum(grad_gated * act, axis=(2, 3)), ("row", "col"))
    grad_epre = grad_excite * excite * (1.0 - excite)
    grad_wexc = jnp.einsum("bs,be->se", squeezed, grad_epre, precision=HIGH)
    grad_spre = jnp.einsum("be,se->bs", grad_epre, w_excite, precision=HIGH) * silu_slope(
        squeeze_pre
    )
    grad_wsq = jnp.einsum("be,bs->es", pooled, grad_spre, precision=HIGH)
    grad_pooled = jnp.einsum("bs,es->be", grad_spre, w_squeeze, precision=HIGH)
    grad_act = grad_gated * excite[:, :, None, None] + (grad_pooled / pixels)[:, :, None, None]
    grad_conv = (grad_act * silu_slope(conv)).astype(jnp.bfloat16)
    grad_pad = with_halo(grad_conv, (("row", 2), ("col", 3)), 1)
    grad_hidden = jnp.zeros(pre.shape, jnp.float32)
    taps = []
    for tap in range(9):
        drow, dcol = (tap // 3, tap % 3)
        grad_hidden = (
            grad_hidden
            + kernel[:, tap][None, :, None, None]
            * grad_pad[:, :, 2 - drow : 2 - drow + rows, 2 - dcol : 2 - dcol + cols]
        )
        taps.append(
            jnp.sum(
                grad_conv.astype(jnp.float32)
                * hidden_pad[:, :, drow : drow + rows, dcol : dcol + cols].astype(jnp.float32),
                axis=(0, 2, 3),
            )
        )
    grad_kernel = jnp.stack(taps, axis=1)
    grad_pre = (grad_hidden * silu_slope(pre)).astype(jnp.bfloat16)
    grad_wexp = jnp.einsum("bchw,behw->ce", scaled, grad_pre, preferred_element_type=jnp.float32)
    grad_scaled = jnp.einsum(
        "ce,behw->bchw", w_expand, grad_pre, preferred_element_type=jnp.float32
    )
    grad_gain = jnp.sum(grad_scaled * normed, axis=(0, 2, 3))
    grad_normed = grad_scaled * norm_gain[None, :, None, None]
    grad_in = inverse * (
        grad_normed - normed * jnp.mean(grad_normed * normed, axis=1, keepdims=True)
    ) + cotangent.astype(jnp.float32)
    grad_wsq_all, grad_wexc_all = lax.psum((grad_wsq, grad_wexc), "dp")
    gain_all, wexp_all, kernel_all, project_all = lax.psum(
        (grad_gain, grad_wexp, grad_kernel, grad_project), ("dp", "row", "col")
    )
    return (
        output,
        grad_in.astype(jnp.bfloat16),
        gain_all,
        wexp_all,
        kernel_all,
        grad_wsq_all,
        grad_wexc_all,
        project_all,
    )


def solution(mesh):
    placed = (
        P("dp", None, "row", "col"),
        P(),
        P(),
        P(),
        P(),
        P(),
        P(),
        P("dp", None, "row", "col"),
    )
    return jax.shard_map(
        local,
        mesh=mesh,
        in_specs=placed,
        out_specs=(
            P("dp", None, "row", "col"),
            P("dp", None, "row", "col"),
            P(),
            P(),
            P(),
            P(),
            P(),
            P(),
        ),
        check_vma=False,
    )
```

profile of v0, /device:TPU:2, one launch (start us, length us, event | category | flops | bytes accessed | tf_op | source)
XLA Modules:
  0.0 487.3 jit_solution(15300703473995289829)
XLA Ops:
  7.2 1.1 fusion.59
  8.4 3.8 fusion.30
  12.2 3.4 collective-permute-start
  15.6 2.5 collective-permute-start.1
  18.1 2.7 collective-permute-done
  20.7 3.1 collective-permute-done.1
  23.9 1.3 collective-permute-start.2
  25.2 1.4 collective-permute-start.3
  26.8 3.5 collective-permute-done.3
  31.3 7.2 %fusion.26 = (f32[768]{0:T(1024)S(1)}, f32[768]{0:T(1024)S(1)}, f32[1,768,8,128]{1,3,2,0:T(8,128)}, f32[768,8,128]{0,2,1:T(8,128)}) fusion(bf16[1,768,10,129]{1,3,2,0:T(8,128)(2,1)S(1)} %get-tuple-element.60, f32[768]{0:T(1024)S(1)} %get-tuple-element.41, bf16[1,768,1,128]{1,3,2,0:T(8,128)(2,1)S(1)} %collective-permute-done.1, ...), kind=kOutput, calls=%fused_computation.48 | convolution fusion | flops 329513472 | bytes 19989504 | tf_op jit(solution)/shard_map/bchw,ec->behw/dot_general | solution.py:69
  38.5 57.0 %all-reduce.2 = (f32[1,768]{1,0:T(1,128)S(1)}, f32[1,768]{1,0:T(1,128)S(1)}) all-reduce(f32[1,768]{1,0:T(1,128)S(1)} %reduce_sum.132, f32[1,768]{1,0:T(1,128)S(1)} %reduce_sum.134), channel_id=1, replica_groups=mesh['dp'=8,'row'=8,'col'=4] {'row','col'}, use_global_device_ids=true, to_apply=%region_2.3 | all-reduce | flops 1536 | bytes 12288 | tf_op jit(solution)/shard_map/psum | solution.py:61
  96.1 3.9 fusion.46
  100.0 1.9 convolution_bitcast_fusion.1
  103.4 5.6 %fusion.24 = (f32[768]{0:T(1024)S(1)}, f32[768]{0:T(1024)S(1)}, f32[768]{0:T(1024)S(1)}, f32[768]{0:T(1024)S(1)}, f32[768]{0:T(1024)S(1)}, /*index=5*/f32[768]{0...) fusion(bf16[1,768,10,129]{1,3,2,0:T(8,128)(2,1)S(1)} %copy-done.4, ...), kind=kLoop, calls=%fused_computation.44 | loop fusion | flops 32236800 | bytes 20874240 | tf_op jit(solution)/shard_map/reduce_sum | solution.py:94
  109.0 2.1 collective-permute-start.4
  111.1 11.1 %collective-permute-start.5 = (bf16[1,768,1,128]{1,3,2,0:T(8,128)(2,1)S(1)}, bf16[1,768,1,128]{1,3,2,0:T(8,128)(2,1)S(1)}, u32[]{:S(2)}, u32[]{:S(2)}) collective-permute-start(bf16[1,768,1,128]{1,3,2,0:T(8,128)(2,1)S(1)} %get-tuple-element.64), channel_id=1, source_target_pairs={{4,0},{8,4},{12,8},{16,12},{20,16},{24,20},{28,24},{5,1},{9,5},{13... | collective-permute-start | bytes 589832 | tf_op jit(solution)/shard_map/ppermute | solution.py:18
  122.9 1.0 collective-permute-done.4
  123.8 1.5 collective-permute-done.5
  125.4 1.3 collective-permute-start.6
  126.7 3.0 collective-permute-start.7
  130.5 1.0 copy.24
  133.8 4.7 fusion.15
  138.5 1.1 copy-done.12
  139.7 1.4 fusion.43
  141.1 2.2 fusion.58
  143.5 1.0 copy.25
  144.5 81.3 %all-reduce = (f32[192]{0:T(256)}, f32[768,9]{0,1:T(8,128)}) all-reduce(f32[192]{0:T(256)S(1)} %get-tuple-element.32, f32[768,9]{0,1:T(8,128)S(1)} %stack.39), channel_id=1, replica_groups=mesh['dp'=8,'row'=8,'col'=4] {'dp','row','col'}, use_global_device_ids=true, to_apply=%region_7.8 | all-reduce | flops 7104 | bytes 56832 | tf_op jit(solution)/shard_map/psum | solution.py:112
  225.8 247.7 %all-reduce.7.cloned.1.call-done = (f32[192,768]{1,0:T(8,128)}, f32[768,192]{0,1:T(8,128)}) async-done(((f32[192,768]{1,0:T(8,128)}, f32[768,192]{0,1:T(8,128)}), (f32[192,768]{1,0:T(8,128)}, f32[768,192]{0,1:T(8,128)})) %all-reduce.7.cloned.1.call-update) | async-done | bytes 1179664 | tf_op jit(solution)/shard_map/psum | solution.py:112
  473.5 1.9 copy.51
  475.4 1.6 copy.52
  477.0 1.6 copy.53
  478.6 1.9 copy.54
  (84 shorter events, 7.0 us)
Async XLA Ops:
  7.2 24.1 %copy-start = (bf16[768,192]{0,1:T(8,128)(2,1)S(1)}, bf16[768,192]{0,1:T(8,128)(2,1)}, u32[]{:S(2)}) copy-start(bf16[768,192]{0,1:T(8,128)(2,1)} %param.14) | copy-start | bytes 884740
  7.2 218.6 %all-reduce.9.cloned.1.call-start = ((), (), s32[]{:S(2)}) async-start(), calls=%async_computation.1 | async-start | bytes 589824 | tf_op jit(solution)/shard_map/psum | solution.py:111
  8.4 18.3 %copy-start.20 = (f32[768,9]{0,1:T(8,128)S(1)}, f32[768,9]{0,1:T(8,128)}, u32[]{:S(2)}) copy-start(f32[768,9]{0,1:T(8,128)} %param.11) | copy-start | bytes 82948
  12.2 8.5 %collective-permute-start = (bf16[1,768,1,128]{1,3,2,0:T(8,128)(2,1)S(1)}, bf16[1,768,1,128]{1,3,2,0:T(8,128)(2,1)S(1)}, u32[]{:S(2)}, u32[]{:S(2)}) collective-permute-start(bf16[1,768,1,128]{1,3,2,0:T(8,128)(2,1)S(1)} %get-tuple-element.65), channel_id=1, source_target_pairs={{0,4},{4,8},{8,12},{12,16},{16,20},{20,24},{24,28},{1,5},{5,9},{9,... | collective-permute-start | bytes 589832 | tf_op jit(solution)/shard_map/ppermute | solution.py:17
  15.6 8.3 %collective-permute-start.1 = (bf16[1,768,1,128]{1,3,2,0:T(8,128)(2,1)S(1)}, bf16[1,768,1,128]{1,3,2,0:T(8,128)(2,1)S(1)}, u32[]{:S(2)}, u32[]{:S(2)}) collective-permute-start(bf16[1,768,1,128]{1,3,2,0:T(8,128)(2,1)S(1)} %get-tuple-element.66), channel_id=1, source_target_pairs={{4,0},{8,4},{12,8},{16,12},{20,16},{24,20},{28,24},{5,1},{9,5},{13... | collective-permute-start | bytes 589832 | tf_op jit(solution)/shard_map/ppermute | solution.py:18
  20.7 10.5 %copy-start.8 = (bf16[1,768,1,128]{1,3,2,0:T(8,128)(2,1)}, bf16[1,768,1,128]{1,3,2,0:T(8,128)(2,1)S(1)}, u32[]{:S(2)}) copy-start(bf16[1,768,1,128]{1,3,2,0:T(8,128)(2,1)S(1)} %collective-permute-done) | copy-start | bytes 589828
  23.9 7.3 %copy-start.10 = (bf16[1,768,1,128]{1,3,2,0:T(8,128)(2,1)}, bf16[1,768,1,128]{1,3,2,0:T(8,128)(2,1)S(1)}, u32[]{:S(2)}) copy-start(bf16[1,768,1,128]{1,3,2,0:T(8,128)(2,1)S(1)} %collective-permute-done.1) | copy-start | bytes 589828
  23.9 2.8 collective-permute-start.2
  25.2 6.0 %copy-start.17 = (bf16[1,192,8,128]{3,2,1,0:T(8,128)(2,1)S(1)}, bf16[1,192,8,128]{3,2,1,0:T(8,128)(2,1)}, u32[]{:S(2)}) copy-start(bf16[1,192,8,128]{3,2,1,0:T(8,128)(2,1)} %param.15) | copy-start | bytes 1179652
  25.2 5.0 %collective-permute-start.3 = (bf16[1,768,10,1]{1,3,2,0:T(2,128)(2,1)S(1)}, bf16[1,768,10,1]{1,3,2,0:T(2,128)(2,1)S(1)}, u32[]{:S(2)}, u32[]{:S(2)}) collective-permute-start(bf16[1,768,10,1]{1,3,2,0:T(2,128)(2,1)S(1)} %get-tuple-element.62), channel_id=1, source_target_pairs={{1,0},{2,1},{3,2},{5,4},{6,5},{7,6},{9,8},{10,9},{11,10},{13,12},{... | collective-permute-start | bytes 46088 | tf_op jit(solution)/shard_map/ppermute | solution.py:18
  31.2 7.3 %copy-start.1 = (bf16[1,768,10,129]{1,3,2,0:T(8,128)(2,1)}, bf16[1,768,10,129]{1,3,2,0:T(8,128)(2,1)S(1)}, u32[]{:S(2)}) copy-start(bf16[1,768,10,129]{1,3,2,0:T(8,128)(2,1)S(1)} %get-tuple-element.59) | copy-start | bytes 5944324
  31.2 7.3 %copy-start.3 = (bf16[1,768,10,129]{1,3,2,0:T(8,128)(2,1)}, bf16[1,768,10,129]{1,3,2,0:T(8,128)(2,1)S(1)}, u32[]{:S(2)}) copy-start(bf16[1,768,10,129]{1,3,2,0:T(8,128)(2,1)S(1)} %get-tuple-element.60) | copy-start | bytes 5944324
  31.2 64.3 %copy-start.16 = (f32[768,48]{0,1:T(8,128)S(1)}, f32[768,48]{0,1:T(8,128)}, u32[]{:S(2)}) copy-start(f32[768,48]{0,1:T(8,128)} %param.12) | copy-start | bytes 442372
  31.3 64.5 %copy-start.15 = (f32[48,768]{1,0:T(8,128)S(1)}, f32[48,768]{1,0:T(8,128)}, u32[]{:S(2)}) copy-start(f32[48,768]{1,0:T(8,128)} %param.13) | copy-start | bytes 442372
  31.3 64.8 %copy-start.13 = (bf16[1,192,8,128]{3,2,1,0:T(8,128)(2,1)S(1)}, bf16[1,192,8,128]{3,2,1,0:T(8,128)(2,1)}, u32[]{:S(2)}) copy-start(bf16[1,192,8,128]{3,2,1,0:T(8,128)(2,1)} %param.8) | copy-start | bytes 1179652
  96.1 3.9 copy-start.6
  100.0 2.5 copy-start.2
  100.0 2.5 copy-start.4
  100.0 3.4 copy-start.7
  100.0 3.4 copy-start.9
  100.0 3.4 copy-start.11
  109.0 21.6 %copy-start.19 = (bf16[1,192,8,128]{3,1,2,0:T(8,128)(2,1)S(1)}, bf16[1,192,8,128]{3,1,2,0:T(8,128)(2,1)}, u32[]{:S(2)}) copy-start(bf16[1,192,8,128]{3,1,2,0:T(8,128)(2,1)} %fusion.46) | copy-start | bytes 1179652
  109.0 14.8 %collective-permute-start.4 = (bf16[1,768,1,128]{1,3,2,0:T(8,128)(2,1)S(1)}, bf16[1,768,1,128]{1,3,2,0:T(8,128)(2,1)S(1)}, u32[]{:S(2)}, u32[]{:S(2)}) collective-permute-start(bf16[1,768,1,128]{1,3,2,0:T(8,128)(2,1)S(1)} %get-tuple-element.63), channel_id=1, source_target_pairs={{0,4},{4,8},{8,12},{12,16},{16,20},{20,24},{24,28},{1,5},{5,9},{9,... | collective-permute-start | bytes 589832 | tf_op jit(solution)/shard_map/ppermute | solution.py:17
  111.1 14.2 %collective-permute-start.5 = (bf16[1,768,1,128]{1,3,2,0:T(8,128)(2,1)S(1)}, bf16[1,768,1,128]{1,3,2,0:T(8,128)(2,1)S(1)}, u32[]{:S(2)}, u32[]{:S(2)}) collective-permute-start(bf16[1,768,1,128]{1,3,2,0:T(8,128)(2,1)S(1)} %get-tuple-element.64), channel_id=1, source_target_pairs={{4,0},{8,4},{12,8},{16,12},{20,16},{24,20},{28,24},{5,1},{9,5},{13... | collective-permute-start | bytes 589832 | tf_op jit(solution)/shard_map/ppermute | solution.py:18
  125.4 6.5 %collective-permute-start.6 = (bf16[1,768,10,1]{1,3,2,0:T(2,128)(2,1)S(1)}, bf16[1,768,10,1]{1,3,2,0:T(2,128)(2,1)S(1)}, u32[]{:S(2)}, u32[]{:S(2)}) collective-permute-start(bf16[1,768,10,1]{1,3,2,0:T(2,128)(2,1)S(1)} %get-tuple-element.57), channel_id=1, source_target_pairs={{1,0},{2,1},{3,2},{5,4},{6,5},{7,6},{9,8},{10,9},{11,10},{13,12},{... | collective-permute-start | bytes 46088 | tf_op jit(solution)/shard_map/ppermute | solution.py:18
  126.7 5.2 %collective-permute-start.7 = (bf16[1,768,10,1]{1,3,2,0:T(2,128)(2,1)S(1)}, bf16[1,768,10,1]{1,3,2,0:T(2,128)(2,1)S(1)}, u32[]{:S(2)}, u32[]{:S(2)}) collective-permute-start(bf16[1,768,10,1]{1,3,2,0:T(2,128)(2,1)S(1)} %get-tuple-element.58), channel_id=1, source_target_pairs={{0,1},{1,2},{2,3},{4,5},{5,6},{6,7},{8,9},{9,10},{10,11},{12,13},{... | collective-permute-start | bytes 46088 | tf_op jit(solution)/shard_map/ppermute | solution.py:17
  131.6 341.9 %all-reduce.7.cloned.1.call-start = ((), (), s32[]{:S(2)}) async-start(), calls=%async_computation | async-start | bytes 2359296 | tf_op jit(solution)/shard_map/psum | solution.py:112
  131.9 1.9 copy-start.5
  133.8 5.9 %copy-start.14 = (bf16[1,192,8,128]{3,2,1,0:T(8,128)(2,1)S(1)}, bf16[1,192,8,128]{3,2,1,0:T(8,128)(2,1)}, u32[]{:S(2)}) copy-start(bf16[1,192,8,128]{3,2,1,0:T(8,128)(2,1)} %param.8) | copy-start | bytes 1179652
  133.8 5.9 %copy-start.21 = (f32[192]{0:T(256)S(1)}, f32[192]{0:T(256)}, u32[]{:S(2)}) copy-start(f32[192]{0:T(256)} %param.9) | copy-start | bytes 2308
  139.7 1.4 copy-start.22
  139.7 3.6 copy-start.18
  (1 other events, 1.2 us)
Sparse Core Ops, SparseCore 0:
  131.7 75.7 all-reduce.8
  213.6 259.8 all-reduce.6
where the time goes:
time: 488 us; the launch traced here: 487 us
  waiting for transfers between devices  259 us (53%)
  blocking collectives  138 us (28%)
  starting transfers between devices  26.3 us (5%)
  matrix products  21.3 us (4%)
  other arithmetic  15.1 us (3%)
  between operations  14.5 us (3%)
  local copies, waits for them, and re-layouts  12.4 us (3%)
    psum x1, waiting for transfers between devices, local(): lax.psum((grad_gain, grad_wexp, grad_kernel, grad_project), ('dp', 'row',...  248 us
    psum x1, blocking collectives, local(): lax.psum((grad_gain, grad_wexp, grad_kernel, grad_project), ('dp', 'row',...  81.3 us
    psum x1, blocking collectives, local(): pooled = lax.psum(jnp.sum(act, axis=(2, 3)), ('row', 'col')) / pixels  57 us
    ppermute x4, starting transfers between devices, with_halo(): after = lax.ppermute(leading, axis, down)  16.2 us
    unnamed x52, local copies, waits for them, and re-layouts  12.1 us
    ppermute x4, starting transfers between devices, with_halo(): before = lax.ppermute(last, axis, up)  9.77 us
  transfers between devices with their start and end apart: 10, of which 6 were waited for; matrix products, arithmetic and copies ran while one was open for 3% of the time, Pallas kernels for 0%

commit v1 on v0

--- a/solution.py
+++ b/solution.py
@@ -58,7 +58,7 @@
     hidden_pad = with_halo(hidden, (("row", 2), ("col", 3)), 1)
     conv = depthwise(hidden_pad, kernel, rows, cols)
     act = jax.nn.silu(conv)
-    pooled = lax.psum(jnp.sum(act, axis=(2, 3)), ("row", "col")) / pixels
+    pooled = lax.psum(lax.psum(jnp.sum(act, axis=(2, 3)), "col"), "row") / pixels
     squeeze_pre = jnp.dot(pooled, w_squeeze, precision=HIGH)
     squeezed = jax.nn.silu(squeeze_pre)
     excite_pre = jnp.dot(squeezed, w_excite, precision=HIGH)

time: 488 us -> 519 us (1.064)
  blocking collectives: 138 us -> 166 us
    psum x1 -> x3, blocking collectives: 57 us -> 83.9 us  [the longest x1 55.5 us: local(): lax.psum(jnp.sum(grad_gated * act, axis=(2, 3)), ('row', 'col'))]
    unnamed x52 -> x42, local copies, waits for them, and re-layouts: 12.1 us -> 11.2 us
where the time goes in v1:
time: 519 us; the launch traced here: 518 us
  waiting for transfers between devices  260 us (50%)
  blocking collectives  166 us (32%)
  starting transfers between devices  26.2 us (5%)
  matrix products  21.3 us (4%)
  other arithmetic  18.8 us (4%)
  between operations  14.5 us (3%)
  local copies, waits for them, and re-layouts  11.5 us (2%)
    psum x1, waiting for transfers between devices, local(): lax.psum((grad_gain, grad_wexp, grad_kernel, grad_project), ('dp', 'row',...  248 us
    psum x1, blocking collectives, local(): lax.psum((grad_gain, grad_wexp, grad_kernel, grad_project), ('dp', 'row',...  81.8 us
    psum x1, blocking collectives, local(): lax.psum(jnp.sum(grad_gated * act, axis=(2, 3)), ('row', 'col'))  55.5 us
    psum x1, blocking collectives, local(): lax.psum(lax.psum(jnp.sum(act, axis=(2, 3)), 'col'), 'row') / pixels  20.1 us
    ppermute x4, starting transfers between devices, with_halo(): after = lax.ppermute(leading, axis, down)  16.2 us
    unnamed x42, local copies, waits for them, and re-layouts  11.2 us
  transfers between devices with their start and end apart: 10, of which 6 were waited for; matrix products, arithmetic and copies ran while one was open for 3% of the time, Pallas kernels for 0%

profile of v1, /device:TPU:2, one launch (start us, length us, event | category | flops | bytes accessed | tf_op | source)
XLA Modules:
  0.0 518.3 jit_solution(7538830945950739718)
XLA Ops:
  7.2 1.1 fusion.59
  8.4 3.8 fusion.30
  12.2 3.4 collective-permute-start
  15.6 2.5 collective-permute-start.1
  18.1 2.7 collective-permute-done
  20.7 3.1 collective-permute-done.1
  23.9 1.3 collective-permute-start.2
  25.2 1.4 collective-permute-start.3
  26.8 3.5 collective-permute-done.3
  31.3 7.2 %fusion.26 = (f32[768]{0:T(1024)S(1)}, f32[768]{0:T(1024)S(1)}, f32[1,768,8,128]{1,3,2,0:T(8,128)}, f32[768,8,128]{0,2,1:T(8,128)}) fusion(bf16[1,768,10,129]{1,3,2,0:T(8,128)(2,1)S(1)} %get-tuple-element.58, f32[768]{0:T(1024)S(1)} %get-tuple-element.41, bf16[1,768,1,128]{1,3,2,0:T(8,128)(2,1)S(1)} %collective-permute-done.1, ...), kind=kOutput, calls=%fused_computation.48 | convolution fusion | flops 329513472 | bytes 19989504 | tf_op jit(solution)/shard_map/bchw,ec->behw/dot_general | solution.py:69
  38.5 8.3 %psum.63 = f32[1,768]{1,0:T(1,128)S(1)} all-reduce(f32[1,768]{1,0:T(1,128)S(1)} %reduce_sum.132), channel_id=1, replica_groups=mesh['dp'=8,'row'=8,'col'=4] {'col'}, use_global_device_ids=true, to_apply=%region_2.3 | all-reduce | flops 768 | bytes 6144 | tf_op jit(solution)/shard_map/psum | solution.py:61
  46.8 20.1 %psum.64 = f32[1,768]{1,0:T(1,128)S(1)} all-reduce(f32[1,768]{1,0:T(1,128)S(1)} %psum.63), channel_id=1, replica_groups=mesh['dp'=8,'row'=8,'col'=4] {'row'}, use_global_device_ids=true, to_apply=%region_3.4 | all-reduce | flops 768 | bytes 6144 | tf_op jit(solution)/shard_map/psum | solution.py:61
  67.4 3.9 fusion.46
  71.3 2.0 convolution_bitcast_fusion.1
  73.2 55.5 %psum.65 = f32[1,768]{1,0:T(1,128)S(1)} all-reduce(f32[1,768]{1,0:T(1,128)S(1)} %reduce_sum.134), channel_id=1, replica_groups=mesh['dp'=8,'row'=8,'col'=4] {'row','col'}, use_global_device_ids=true, to_apply=%region_5.6 | all-reduce | flops 768 | bytes 6144 | tf_op jit(solution)/shard_map/psum | solution.py:73
  129.2 9.3 %fusion.24 = (f32[768]{0:T(1024)S(1)}, f32[768]{0:T(1024)S(1)}, f32[768]{0:T(1024)S(1)}, f32[768]{0:T(1024)S(1)}, f32[768]{0:T(1024)S(1)}, /*index=5*/f32[768]{0...) fusion(bf16[1,768,10,129]{1,3,2,0:T(8,128)(2,1)} %copy-done.2, ...), kind=kLoop, calls=%fused_computation.44 | loop fusion | flops 32236800 | bytes 20874240 | tf_op jit(solution)/shard_map/reduce_sum | solution.py:94
  138.6 2.1 collective-permute-start.4
  140.7 11.0 %collective-permute-start.5 = (bf16[1,768,1,128]{1,3,2,0:T(8,128)(2,1)S(1)}, bf16[1,768,1,128]{1,3,2,0:T(8,128)(2,1)S(1)}, u32[]{:S(2)}, u32[]{:S(2)}) collective-permute-start(bf16[1,768,1,128]{1,3,2,0:T(8,128)(2,1)S(1)} %get-tuple-element.62), channel_id=1, source_target_pairs={{4,0},{8,4},{12,8},{16,12},{20,16},{24,20},{28,24},{5,1},{9,5},{13... | collective-permute-start | bytes 589832 | tf_op jit(solution)/shard_map/ppermute | solution.py:18
  152.4 2.2 collective-permute-done.4
  154.6 1.2 collective-permute-done.5
  155.9 1.3 collective-permute-start.6
  157.2 3.0 collective-permute-start.7
  164.3 4.7 fusion.15
  169.0 1.1 copy-done.7
  170.2 1.3 fusion.43
  171.6 2.2 fusion.58
  175.0 81.8 %all-reduce = (f32[192]{0:T(256)}, f32[768,9]{0,1:T(8,128)}) all-reduce(f32[192]{0:T(256)S(1)} %get-tuple-element.32, f32[768,9]{0,1:T(8,128)S(1)} %stack.39), channel_id=1, replica_groups=mesh['dp'=8,'row'=8,'col'=4] {'dp','row','col'}, use_global_device_ids=true, to_apply=%region_8.9 | all-reduce | flops 7104 | bytes 56832 | tf_op jit(solution)/shard_map/psum | solution.py:112
  256.8 247.7 %all-reduce.6.cloned.1.call-done = (f32[192,768]{1,0:T(8,128)}, f32[768,192]{0,1:T(8,128)}) async-done(((f32[192,768]{1,0:T(8,128)}, f32[768,192]{0,1:T(8,128)}), (f32[192,768]{1,0:T(8,128)}, f32[768,192]{0,1:T(8,128)})) %all-reduce.6.cloned.1.call-update) | async-done | bytes 1179664 | tf_op jit(solution)/shard_map/psum | solution.py:112
  504.5 1.9 copy.51
  506.4 1.6 copy.52
  508.0 1.6 copy.53
  509.6 1.9 copy.54
  (77 shorter events, 8.2 us)
Async XLA Ops:
  7.2 24.1 %copy-start = (bf16[768,192]{0,1:T(8,128)(2,1)S(1)}, bf16[768,192]{0,1:T(8,128)(2,1)}, u32[]{:S(2)}) copy-start(bf16[768,192]{0,1:T(8,128)(2,1)} %param.14) | copy-start | bytes 884740
  7.2 249.6 %all-reduce.8.cloned.1.call-start = ((), (), s32[]{:S(2)}) async-start(), calls=%async_computation.1 | async-start | bytes 589824 | tf_op jit(solution)/shard_map/psum | solution.py:111
  8.4 18.3 %copy-start.15 = (f32[768,9]{0,1:T(8,128)S(1)}, f32[768,9]{0,1:T(8,128)}, u32[]{:S(2)}) copy-start(f32[768,9]{0,1:T(8,128)} %param.11) | copy-start | bytes 82948
  12.2 8.5 %collective-permute-start = (bf16[1,768,1,128]{1,3,2,0:T(8,128)(2,1)S(1)}, bf16[1,768,1,128]{1,3,2,0:T(8,128)(2,1)S(1)}, u32[]{:S(2)}, u32[]{:S(2)}) collective-permute-start(bf16[1,768,1,128]{1,3,2,0:T(8,128)(2,1)S(1)} %get-tuple-element.63), channel_id=1, source_target_pairs={{0,4},{4,8},{8,12},{12,16},{16,20},{20,24},{24,28},{1,5},{5,9},{9,... | collective-permute-start | bytes 589832 | tf_op jit(solution)/shard_map/ppermute | solution.py:17
  15.6 8.3 %collective-permute-start.1 = (bf16[1,768,1,128]{1,3,2,0:T(8,128)(2,1)S(1)}, bf16[1,768,1,128]{1,3,2,0:T(8,128)(2,1)S(1)}, u32[]{:S(2)}, u32[]{:S(2)}) collective-permute-start(bf16[1,768,1,128]{1,3,2,0:T(8,128)(2,1)S(1)} %get-tuple-element.64), channel_id=1, source_target_pairs={{4,0},{8,4},{12,8},{16,12},{20,16},{24,20},{28,24},{5,1},{9,5},{13... | collective-permute-start | bytes 589832 | tf_op jit(solution)/shard_map/ppermute | solution.py:18
  20.7 10.5 %copy-start.5 = (bf16[1,768,1,128]{1,3,2,0:T(8,128)(2,1)}, bf16[1,768,1,128]{1,3,2,0:T(8,128)(2,1)S(1)}, u32[]{:S(2)}) copy-start(bf16[1,768,1,128]{1,3,2,0:T(8,128)(2,1)S(1)} %collective-permute-done) | copy-start | bytes 589828
  23.9 7.3 %copy-start.6 = (bf16[1,768,1,128]{1,3,2,0:T(8,128)(2,1)}, bf16[1,768,1,128]{1,3,2,0:T(8,128)(2,1)S(1)}, u32[]{:S(2)}) copy-start(bf16[1,768,1,128]{1,3,2,0:T(8,128)(2,1)S(1)} %collective-permute-done.1) | copy-start | bytes 589828
  23.9 2.8 collective-permute-start.2
  25.2 6.0 %copy-start.12 = (bf16[1,192,8,128]{3,2,1,0:T(8,128)(2,1)S(1)}, bf16[1,192,8,128]{3,2,1,0:T(8,128)(2,1)}, u32[]{:S(2)}) copy-start(bf16[1,192,8,128]{3,2,1,0:T(8,128)(2,1)} %param.15) | copy-start | bytes 1179652
  25.2 5.0 collective-permute-start.3
  31.2 7.3 %copy-start.1 = (bf16[1,768,10,129]{1,3,2,0:T(8,128)(2,1)}, bf16[1,768,10,129]{1,3,2,0:T(8,128)(2,1)S(1)}, u32[]{:S(2)}) copy-start(bf16[1,768,10,129]{1,3,2,0:T(8,128)(2,1)S(1)} %get-tuple-element.57) | copy-start | bytes 5944324
  31.2 7.3 %copy-start.2 = (bf16[1,768,10,129]{1,3,2,0:T(8,128)(2,1)}, bf16[1,768,10,129]{1,3,2,0:T(8,128)(2,1)S(1)}, u32[]{:S(2)}) copy-start(bf16[1,768,10,129]{1,3,2,0:T(8,128)(2,1)S(1)} %get-tuple-element.58) | copy-start | bytes 5944324
  31.2 35.6 %copy-start.11 = (f32[768,48]{0,1:T(8,128)S(1)}, f32[768,48]{0,1:T(8,128)}, u32[]{:S(2)}) copy-start(f32[768,48]{0,1:T(8,128)} %param.12) | copy-start | bytes 442372
  31.3 35.8 %copy-start.10 = (f32[48,768]{1,0:T(8,128)S(1)}, f32[48,768]{1,0:T(8,128)}, u32[]{:S(2)}) copy-start(f32[48,768]{1,0:T(8,128)} %param.13) | copy-start | bytes 442372
  31.3 36.1 %copy-start.8 = (bf16[1,192,8,128]{3,2,1,0:T(8,128)(2,1)S(1)}, bf16[1,192,8,128]{3,2,1,0:T(8,128)(2,1)}, u32[]{:S(2)}) copy-start(bf16[1,192,8,128]{3,2,1,0:T(8,128)(2,1)} %param.8) | copy-start | bytes 1179652
  67.4 3.9 copy-start.4
  138.5 22.5 %copy-start.14 = (bf16[1,192,8,128]{3,1,2,0:T(8,128)(2,1)S(1)}, bf16[1,192,8,128]{3,1,2,0:T(8,128)(2,1)}, u32[]{:S(2)}) copy-start(bf16[1,192,8,128]{3,1,2,0:T(8,128)(2,1)} %fusion.46) | copy-start | bytes 1179652
  138.6 16.0 %collective-permute-start.4 = (bf16[1,768,1,128]{1,3,2,0:T(8,128)(2,1)S(1)}, bf16[1,768,1,128]{1,3,2,0:T(8,128)(2,1)S(1)}, u32[]{:S(2)}, u32[]{:S(2)}) collective-permute-start(bf16[1,768,1,128]{1,3,2,0:T(8,128)(2,1)S(1)} %get-tuple-element.61), channel_id=1, source_target_pairs={{0,4},{4,8},{8,12},{12,16},{16,20},{20,24},{24,28},{1,5},{5,9},{9,... | collective-permute-start | bytes 589832 | tf_op jit(solution)/shard_map/ppermute | solution.py:17
  140.7 15.2 %collective-permute-start.5 = (bf16[1,768,1,128]{1,3,2,0:T(8,128)(2,1)S(1)}, bf16[1,768,1,128]{1,3,2,0:T(8,128)(2,1)S(1)}, u32[]{:S(2)}, u32[]{:S(2)}) collective-permute-start(bf16[1,768,1,128]{1,3,2,0:T(8,128)(2,1)S(1)} %get-tuple-element.62), channel_id=1, source_target_pairs={{4,0},{8,4},{12,8},{16,12},{20,16},{24,20},{28,24},{5,1},{9,5},{13... | collective-permute-start | bytes 589832 | tf_op jit(solution)/shard_map/ppermute | solution.py:18
  155.9 6.5 %collective-permute-start.6 = (bf16[1,768,10,1]{1,3,2,0:T(2,128)(2,1)S(1)}, bf16[1,768,10,1]{1,3,2,0:T(2,128)(2,1)S(1)}, u32[]{:S(2)}, u32[]{:S(2)}) collective-permute-start(bf16[1,768,10,1]{1,3,2,0:T(2,128)(2,1)S(1)} %get-tuple-element.55), channel_id=1, source_target_pairs={{1,0},{2,1},{3,2},{5,4},{6,5},{7,6},{9,8},{10,9},{11,10},{13,12},{... | collective-permute-start | bytes 46088 | tf_op jit(solution)/shard_map/ppermute | solution.py:18
  157.2 5.2 %collective-permute-start.7 = (bf16[1,768,10,1]{1,3,2,0:T(2,128)(2,1)S(1)}, bf16[1,768,10,1]{1,3,2,0:T(2,128)(2,1)S(1)}, u32[]{:S(2)}, u32[]{:S(2)}) collective-permute-start(bf16[1,768,10,1]{1,3,2,0:T(2,128)(2,1)S(1)} %get-tuple-element.56), channel_id=1, source_target_pairs={{0,1},{1,2},{2,3},{4,5},{5,6},{6,7},{8,9},{9,10},{10,11},{12,13},{... | collective-permute-start | bytes 46088 | tf_op jit(solution)/shard_map/ppermute | solution.py:17
  162.1 342.4 %all-reduce.6.cloned.1.call-start = ((), (), s32[]{:S(2)}) async-start(), calls=%async_computation | async-start | bytes 2359296 | tf_op jit(solution)/shard_map/psum | solution.py:112
  162.4 1.9 copy-start.3
  164.3 5.9 %copy-start.9 = (bf16[1,192,8,128]{3,2,1,0:T(8,128)(2,1)S(1)}, bf16[1,192,8,128]{3,2,1,0:T(8,128)(2,1)}, u32[]{:S(2)}) copy-start(bf16[1,192,8,128]{3,2,1,0:T(8,128)(2,1)} %param.8) | copy-start | bytes 1179652
  164.3 5.9 %copy-start.16 = (f32[192]{0:T(256)S(1)}, f32[192]{0:T(256)}, u32[]{:S(2)}) copy-start(f32[192]{0:T(256)} %param.9) | copy-start | bytes 2308
  169.0 1.2 copy-start.7
  170.2 1.4 copy-start.17
  170.2 3.6 copy-start.13
Sparse Core Ops, SparseCore 0:
  162.2 76.3 all-reduce.7
  244.6 259.8 all-reduce.5
